TPU v7x, 512 devices: a whole 4x4x16 slice. The times are simulated.
512 devices in a mesh: space: 64 (over x, z), node: 4 (over y_hi, core), tm: 2 (over y_lo).
Axes of the slice: x: 4, y: 4 (y_hi: 2, y_lo: 2; y = y_hi * 2 + y_lo), z: 16, core: 2. Of those that a mesh axis runs over, the one named last changes fastest.
Arguments:
- start_old: float32 [2, 512, 128, 256], P('tm', 'space'), may hold values from -4 to 4
- nodes_old: float32 [2, 4, 512, 128, 256], P('tm', 'node', 'space'), may hold values from -4 to 4
Outputs:
- nodes_new: float32 [2, 4, 512, 128, 256], P('tm', 'node', 'space')
- end_new: float32 [2, 512, 128, 256], P('tm', 'space')
All inputs are finite; a program needn't handle non-finite values.
Results may differ from a plain program's by a relative error of at most 0.00002.
Values sent between devices are 32-bit elements; how exact they have to be, the bound alone decides.
A program may use at most 64 MiB of HBM per device.

v0:
```python
import jax
import jax.numpy as jnp
from jax import lax
from jax.sharding import PartitionSpec as P

NODES = 4
PASSES = 4
time_step = 0.25
diffusion = 4.0
reaction = 1.0


def padded_2(block, sides, width):
    for axis, dim in sides:
        count = lax.axis_size(axis)
        forward = [(i, i + 1) for i in range(count - 1)]
        forward.append((count - 1, 0))
        backward = [(target, source) for source, target in forward]
        low = lax.ppermute(
            lax.slice_in_dim(block, block.shape[dim] - width, None, axis=dim), axis, forward
        )
        high = lax.ppermute(lax.slice_in_dim(block, 0, width, axis=dim), axis, backward)
        block = jnp.concatenate([low, block, high], axis=dim)
    return block


def shifted_2(array, axis, by):
    size = lax.axis_size(axis)
    pairs = [(i, i + by) for i in range(size) if 0 <= i + by < size]
    return lax.ppermute(array, axis, pairs)


def collocation(count):
    points = [-0.8611363115940526, -0.3399810435848563, 0.3399810435848563, 0.8611363115940526]
    raw_weights = [0.3478548451374538, 0.6521451548625461, 0.6521451548625461, 0.3478548451374538]
    node_times = [(point + 1.0) / 2.0 for point in points]
    quadrature = [[0.0 for column in range(count)] for target in range(count)]
    for source in range(count):
        coeffs = [1.0]
        scaling = 1.0
        for other in range(count):
            if other != source:
                other_time = node_times[other]
                shifted = [0.0] + coeffs
                for power in range(len(coeffs)):
                    shifted[power] = shifted[power] - other_time * coeffs[power]
                coeffs = shifted
                scaling = scaling * (node_times[source] - other_time)
        for target in range(count):
            target_time = node_times[target]
            integral = 0.0
            for power in range(len(coeffs)):
                integral = integral + coeffs[power] * target_time ** (power + 1) / (power + 1)
            quadrature[target][source] = integral / scaling
    return (node_times, quadrature, [weight / 2.0 for weight in raw_weights])


def neighbour_sum(padded):
    inner = padded[1:-1]
    total = padded[2:] + padded[:-2]
    total = total + jnp.roll(inner, -1, 1) + jnp.roll(inner, 1, 1)
    total = total + jnp.roll(inner, -1, 2) + jnp.roll(inner, 1, 2)
    return total


def forcing(values, padded):
    laplace = neighbour_sum(padded) - 6.0 * values
    return (laplace, diffusion * laplace + reaction * (values - values * values * values))


def on_device(start_old, nodes_old):
    node_times, quadrature, weights = collocation(NODES)
    node_index = lax.axis_index("node")
    node_time = jnp.asarray(node_times, jnp.float32)[node_index]
    weight_table = jnp.asarray(weights, jnp.float32)
    node_weight = weight_table[node_index]
    quad_table = jnp.asarray(quadrature, jnp.float32)
    state_old = nodes_old[0, 0]
    start_state = start_old[0]
    padded = padded_2(state_old, (("space", 0),), 1)
    laplace_old, force_old = forcing(state_old, padded)
    quad_row = quad_table[node_index]
    shard_piece = lax.all_gather(force_old[None], "node", axis=0, tiled=True)
    quad_part = jnp.sum(quad_row[:, None, None, None] * shard_piece, axis=0)
    weight_part = jnp.sum(weight_table[:, None, None, None] * shard_piece, axis=0)
    end_old = start_state + time_step * weight_part
    received = shifted_2(end_old, "tm", 1)
    begin_state = jnp.where(lax.axis_index("tm") == 0, start_state, received)
    implicit = time_step * diffusion * node_time
    right_side = begin_state + time_step * quad_part - implicit * laplace_old
    divisor = 1.0 + 6.0 * implicit
    iterate = state_old
    for step_index in range(PASSES):
        widened = padded_2(iterate, (("space", 0),), 1)
        iterate = (right_side + implicit * neighbour_sum(widened)) / divisor
    padded_new = padded_2(iterate, (("space", 0),), 1)
    laplace_new, force_new = forcing(iterate, padded_new)
    weighted_new = lax.psum(node_weight * force_new, "node")
    end_new = begin_state + time_step * weighted_new
    return (iterate[None, None], end_new[None])


def solution(mesh):
    return jax.shard_map(
        on_device,
        mesh=mesh,
        in_specs=(P("tm", "space", None, None), P("tm", "node", "space", None, None)),
        out_specs=(P("tm", "node", "space", None, None), P("tm", "space", None, None)),
        check_vma=False,
    )
```

profile of v0, /device:TPU:1, one launch (start us, length us, event | category | flops | bytes accessed | tf_op | source)
XLA Modules:
  0.0 228.6 jit_solution(15902153033855880192)
XLA Ops:
  7.2 1.1 slice_bitcast_fusion.1
  8.3 14.1 %collective-permute-start = (f32[1,128,256]{2,1,0:T(8,128)S(1)}, f32[1,128,256]{2,1,0:T(8,128)S(1)}, u32[]{:S(2)}, u32[]{:S(2)}) collective-permute-start(f32[1,128,256]{2,1,0:T(8,128)S(1)} %get-tuple-element.48), channel_id=1, source_target_pairs={{8,0},{16,8},{24,16},{32,24},{40,32},{48,40},{56,48},{64,56},{72,6... | collective-permute-start | bytes 393224 | tf_op jit(solution)/shard_map/ppermute | solution.py:22
  22.4 1.9 collective-permute-start.1
  24.4 1.4 fusion.63
  25.8 1.9 fusion.62
  27.9 3.5 %collective-permute-done.1 = f32[1,128,256]{2,1,0:T(8,128)S(1)} collective-permute-done((f32[1,128,256]{2,1,0:T(8,128)S(1)}, f32[1,128,256]{2,1,0:T(8,128)S(1)}, u32[]{:S(2)}, u32[]{:S(2)}) %collective-permute-start.1) | collective-permute-done | bytes 131104 | tf_op jit(solution)/shard_map/ppermute | solution.py:19
  31.5 2.2 fusion
  33.8 0.8 dynamic-slice_bitcast_fusion
  34.5 38.3 %all-gather.3.cloned.1.call-done = f32[32,128,256]{2,1,0:T(8,128)} async-done(((f32[8,128,256]{2,1,0:T(8,128)}), f32[32,128,256]{2,1,0:T(8,128)}) %all-gather.3.cloned.1.call-update) | async-done | bytes 4194320 | tf_op jit(solution)/shard_map/all_gather | solution.py:83
  72.8 4.1 %multiply_reduce_fusion.1 = (f32[8,128,256]{2,1,0:T(8,128)S(1)}, f32[8,128,256]{2,1,0:T(8,128)}) fusion(f32[4,8,128,256]{3,2,1,0:T(8,128)} %bitcast.30, f32[4]{0:T(128)S(1)} %copy-done.3, f32[4]{0:T(128)S(1)} %dynamic-slice_bitcast_fusion), kind=kLoop, calls=%fused_computation.1 | loop fusion | flops 3670016 | bytes 6291488 | tf_op jit(solution)/shard_map/reduce_sum | solution.py:85
  76.9 1.1 bitcast_add_fusion
  78.0 2.3 collective-permute-start.2
  82.1 20.7 %collective-permute-done.2 = f32[8,128,256]{2,1,0:T(8,128)S(1)} collective-permute-done((f32[8,128,256]{2,1,0:T(8,128)}, f32[8,128,256]{2,1,0:T(8,128)S(1)}, u32[]{:S(2)}, u32[]{:S(2)}) %collective-permute-start.2) | collective-permute-done | bytes 1048608 | tf_op jit(solution)/shard_map/ppermute | solution.py:30
  102.8 2.5 %add_divide_fusion = (f32[8,128,256]{2,1,0:T(8,128)S(1)}, f32[8,128,256]{2,1,0:T(8,128)S(1)}) fusion(f32[8,128,256]{2,1,0:T(8,128)} %get-tuple-element.7, f32[]{:T(128)S(6)} %add.127, f32[]{:T(128)} %bitcast.6, f32[1,1,8,128,256]{4,3,2,1,0:T(8,128)S(1)} %copy-done, f32[8,128,256]{2,1,0:T(8,128)} %get-tuple-element.3, ...), kind=kLoop, calls=%fused_computation.56 | loop fusion | flops 2621440 | bytes 7340041 | tf_op jit(solution)/shard_map/div | solution.py:95
  106.0 7.8 %collective-permute-start.3 = (f32[1,128,256]{2,1,0:T(8,128)S(1)}, f32[1,128,256]{2,1,0:T(8,128)S(1)}, u32[]{:S(2)}, u32[]{:S(2)}) collective-permute-start(f32[1,128,256]{2,1,0:T(8,128)S(1)} %get-tuple-element.46), channel_id=1, source_target_pairs={{8,0},{16,8},{24,16},{32,24},{40,32},{48,40},{56,48},{64,56},{72,6... | collective-permute-start | bytes 393224 | tf_op jit(solution)/shard_map/ppermute | solution.py:22
  113.9 1.9 collective-permute-start.4
  115.8 7.1 %collective-permute-done.4 = f32[1,128,256]{2,1,0:T(8,128)S(1)} collective-permute-done((f32[1,128,256]{2,1,0:T(8,128)S(1)}, f32[1,128,256]{2,1,0:T(8,128)S(1)}, u32[]{:S(2)}, u32[]{:S(2)}) %collective-permute-start.4) | collective-permute-done | bytes 131104 | tf_op jit(solution)/shard_map/ppermute | solution.py:19
  122.9 1.2 fusion.33
  124.9 1.9 collective-permute-start.5
  126.8 3.4 %collective-permute-start.6 = (f32[1,128,256]{2,1,0:T(8,128)S(1)}, f32[1,128,256]{2,1,0:T(8,128)S(1)}, u32[]{:S(2)}, u32[]{:S(2)}) collective-permute-start(f32[1,128,256]{2,1,0:T(8,128)S(1)} %get-tuple-element.37), channel_id=1, source_target_pairs={{0,8},{8,16},{16,24},{24,32},{32,40},{40,48},{48,56},{56,64},{64,7... | collective-permute-start | bytes 393224 | tf_op jit(solution)/shard_map/ppermute | solution.py:19
  130.6 5.2 %collective-permute-done.6 = f32[1,128,256]{2,1,0:T(8,128)S(1)} collective-permute-done((f32[1,128,256]{2,1,0:T(8,128)S(1)}, f32[1,128,256]{2,1,0:T(8,128)S(1)}, u32[]{:S(2)}, u32[]{:S(2)}) %collective-permute-start.6) | collective-permute-done | bytes 131104 | tf_op jit(solution)/shard_map/ppermute | solution.py:19
  135.9 1.2 fusion.25
  137.9 1.9 collective-permute-start.7
  139.8 3.4 %collective-permute-start.8 = (f32[1,128,256]{2,1,0:T(8,128)S(1)}, f32[1,128,256]{2,1,0:T(8,128)S(1)}, u32[]{:S(2)}, u32[]{:S(2)}) collective-permute-start(f32[1,128,256]{2,1,0:T(8,128)S(1)} %get-tuple-element.27), channel_id=1, source_target_pairs={{0,8},{8,16},{16,24},{24,32},{32,40},{40,48},{48,56},{56,64},{64,7... | collective-permute-start | bytes 393224 | tf_op jit(solution)/shard_map/ppermute | solution.py:19
  143.6 5.2 %collective-permute-done.8 = f32[1,128,256]{2,1,0:T(8,128)S(1)} collective-permute-done((f32[1,128,256]{2,1,0:T(8,128)S(1)}, f32[1,128,256]{2,1,0:T(8,128)S(1)}, u32[]{:S(2)}, u32[]{:S(2)}) %collective-permute-start.8) | collective-permute-done | bytes 131104 | tf_op jit(solution)/shard_map/ppermute | solution.py:19
  148.8 1.2 fusion.17
  150.9 1.9 collective-permute-start.9
  152.8 3.4 %collective-permute-start.10 = (f32[1,128,256]{2,1,0:T(8,128)S(1)}, f32[1,128,256]{2,1,0:T(8,128)S(1)}, u32[]{:S(2)}, u32[]{:S(2)}) collective-permute-start(f32[1,128,256]{2,1,0:T(8,128)S(1)} %get-tuple-element.17), channel_id=1, source_target_pairs={{0,8},{8,16},{16,24},{24,32},{32,40},{40,48},{48,56},{56,64},{64,7... | collective-permute-start | bytes 393224 | tf_op jit(solution)/shard_map/ppermute | solution.py:19
  156.6 5.2 %collective-permute-done.10 = f32[1,128,256]{2,1,0:T(8,128)S(1)} collective-permute-done((f32[1,128,256]{2,1,0:T(8,128)S(1)}, f32[1,128,256]{2,1,0:T(8,128)S(1)}, u32[]{:S(2)}, u32[]{:S(2)}) %collective-permute-start.10) | collective-permute-done | bytes 131104 | tf_op jit(solution)/shard_map/ppermute | solution.py:19
  161.8 2.4 %fusion.2 = f32[8,128,256]{2,1,0:T(8,128)} fusion(f32[8,128,256]{2,1,0:T(8,128)S(1)} %fusion.17, f32[1,128,256]{2,1,0:T(8,128)S(1)} %collective-permute-done.10, f32[1,128,256]{2,1,0:T(8,128)S(1)} %collective-permute-done.9, f32[8,1,256]{2,1,0:T(1,128)S(1)} %get-tuple-element.13, f32[8,127,256]{2,1,0:T(8,128)S(1)} %get-tuple-element.15, ...), kind=kLoop, calls=%fused_computation.6 | loop fusion | flops 4980736 | bytes 6553604 | tf_op jit(solution)/shard_map/mul | solution.py:98
  164.3 55.1 %all-reduce.2.cloned.1.call-done = f32[8,128,256]{2,1,0:T(8,128)} async-done(((f32[8,128,256]{2,1,0:T(8,128)}), f32[8,128,256]{2,1,0:T(8,128)}) %all-reduce.2.cloned.1.call-update) | async-done | bytes 1048592 | tf_op jit(solution)/shard_map/psum | solution.py:98
  219.4 2.4 %add_bitcast_fusion = f32[1,8,128,256]{3,2,1,0:T(8,128)} fusion(f32[8,128,256]{2,1,0:T(8,128)} %all-reduce.2.cloned.1.call-done, f32[8,128,256]{2,1,0:T(8,128)S(1)} %collective-permute-done.2, f32[1,8,128,256]{3,2,1,0:T(8,128)S(1)} %copy-done.2, pred[]{:T(512)S(6)} %eq.3), kind=kLoop, calls=%fused_computation.55 | loop fusion | flops 786432 | bytes 4194305 | tf_op jit(solution)/shard_map/broadcast_in_dim | solution.py:100
  (43 shorter events, 5.9 us)
Async XLA Ops:
  7.2 20.5 %copy-start = (f32[1,1,8,128,256]{4,3,2,1,0:T(8,128)S(1)}, f32[1,1,8,128,256]{4,3,2,1,0:T(8,128)}, u32[]{:S(2)}) copy-start(f32[1,1,8,128,256]{4,3,2,1,0:T(8,128)} %param.6) | copy-start | bytes 3145732
  7.2 65.7 %all-gather.3.cloned.1.call-start = ((), (), s32[]{:S(2)}) async-start(), calls=%async_computation.1 | async-start | bytes 5242880 | tf_op jit(solution)/shard_map/all_gather | solution.py:83
  8.3 19.6 %collective-permute-start = (f32[1,128,256]{2,1,0:T(8,128)S(1)}, f32[1,128,256]{2,1,0:T(8,128)S(1)}, u32[]{:S(2)}, u32[]{:S(2)}) collective-permute-start(f32[1,128,256]{2,1,0:T(8,128)S(1)} %get-tuple-element.48), channel_id=1, source_target_pairs={{8,0},{16,8},{24,16},{32,24},{40,32},{48,40},{56,48},{64,56},{72,6... | collective-permute-start | bytes 393224 | tf_op jit(solution)/shard_map/ppermute | solution.py:22
  22.4 9.0 %collective-permute-start.1 = (f32[1,128,256]{2,1,0:T(8,128)S(1)}, f32[1,128,256]{2,1,0:T(8,128)S(1)}, u32[]{:S(2)}, u32[]{:S(2)}) collective-permute-start(f32[1,128,256]{2,1,0:T(8,128)S(1)} %get-tuple-element.49), channel_id=1, source_target_pairs={{0,8},{8,16},{16,24},{24,32},{32,40},{40,48},{48,56},{56,64},{64,7... | collective-permute-start | bytes 393224 | tf_op jit(solution)/shard_map/ppermute | solution.py:19
  31.5 41.4 %copy-start.3 = (f32[4]{0:T(128)S(1)}, f32[4]{0:T(128)}, u32[]{:S(2)}) copy-start(f32[4]{0:T(128)} %constant.30.clone) | copy-start | bytes 52
  33.7 43.2 %copy-start.2 = (f32[1,8,128,256]{3,2,1,0:T(8,128)S(1)}, f32[1,8,128,256]{3,2,1,0:T(8,128)}, u32[]{:S(2)}) copy-start(f32[1,8,128,256]{3,2,1,0:T(8,128)} %param.5) | copy-start | bytes 3145732
  33.7 185.7 %all-reduce.2.cloned.1.call-start = ((), (), s32[]{:S(2)}) async-start(), calls=%async_computation | async-start | bytes 2097152 | tf_op jit(solution)/shard_map/psum | solution.py:98
  72.8 8.1 %copy-start.4 = (f32[4]{0:T(128)S(1)}, f32[4]{0:T(128)}, u32[]{:S(2)}) copy-start(f32[4]{0:T(128)} %constant.29.clone) | copy-start | bytes 52
  78.0 24.7 %collective-permute-start.2 = (f32[8,128,256]{2,1,0:T(8,128)}, f32[8,128,256]{2,1,0:T(8,128)S(1)}, u32[]{:S(2)}, u32[]{:S(2)}) collective-permute-start(f32[8,128,256]{2,1,0:T(8,128)} %bitcast_add_fusion), channel_id=1, source_target_pairs={{0,1},{2,3},{4,5},{6,7},{8,9},{10,11},{12,13},{14,15},{16,17},{18,... | collective-permute-start | bytes 3145736 | tf_op jit(solution)/shard_map/ppermute | solution.py:30
  106.0 9.8 %collective-permute-start.3 = (f32[1,128,256]{2,1,0:T(8,128)S(1)}, f32[1,128,256]{2,1,0:T(8,128)S(1)}, u32[]{:S(2)}, u32[]{:S(2)}) collective-permute-start(f32[1,128,256]{2,1,0:T(8,128)S(1)} %get-tuple-element.46), channel_id=1, source_target_pairs={{8,0},{16,8},{24,16},{32,24},{40,32},{48,40},{56,48},{64,56},{72,6... | collective-permute-start | bytes 393224 | tf_op jit(solution)/shard_map/ppermute | solution.py:22
  113.9 9.0 %collective-permute-start.4 = (f32[1,128,256]{2,1,0:T(8,128)S(1)}, f32[1,128,256]{2,1,0:T(8,128)S(1)}, u32[]{:S(2)}, u32[]{:S(2)}) collective-permute-start(f32[1,128,256]{2,1,0:T(8,128)S(1)} %get-tuple-element.47), channel_id=1, source_target_pairs={{0,8},{8,16},{16,24},{24,32},{32,40},{40,48},{48,56},{56,64},{64,7... | collective-permute-start | bytes 393224 | tf_op jit(solution)/shard_map/ppermute | solution.py:19
  124.9 5.7 %collective-permute-start.5 = (f32[1,128,256]{2,1,0:T(8,128)S(1)}, f32[1,128,256]{2,1,0:T(8,128)S(1)}, u32[]{:S(2)}, u32[]{:S(2)}) collective-permute-start(f32[1,128,256]{2,1,0:T(8,128)S(1)} %get-tuple-element.36), channel_id=1, source_target_pairs={{8,0},{16,8},{24,16},{32,24},{40,32},{48,40},{56,48},{64,56},{72,6... | collective-permute-start | bytes 393224 | tf_op jit(solution)/shard_map/ppermute | solution.py:22
  126.8 9.0 %collective-permute-start.6 = (f32[1,128,256]{2,1,0:T(8,128)S(1)}, f32[1,128,256]{2,1,0:T(8,128)S(1)}, u32[]{:S(2)}, u32[]{:S(2)}) collective-permute-start(f32[1,128,256]{2,1,0:T(8,128)S(1)} %get-tuple-element.37), channel_id=1, source_target_pairs={{0,8},{8,16},{16,24},{24,32},{32,40},{40,48},{48,56},{56,64},{64,7... | collective-permute-start | bytes 393224 | tf_op jit(solution)/shard_map/ppermute | solution.py:19
  137.9 5.7 %collective-permute-start.7 = (f32[1,128,256]{2,1,0:T(8,128)S(1)}, f32[1,128,256]{2,1,0:T(8,128)S(1)}, u32[]{:S(2)}, u32[]{:S(2)}) collective-permute-start(f32[1,128,256]{2,1,0:T(8,128)S(1)} %get-tuple-element.26), channel_id=1, source_target_pairs={{8,0},{16,8},{24,16},{32,24},{40,32},{48,40},{56,48},{64,56},{72,6... | collective-permute-start | bytes 393224 | tf_op jit(solution)/shard_map/ppermute | solution.py:22
  139.8 9.0 %collective-permute-start.8 = (f32[1,128,256]{2,1,0:T(8,128)S(1)}, f32[1,128,256]{2,1,0:T(8,128)S(1)}, u32[]{:S(2)}, u32[]{:S(2)}) collective-permute-start(f32[1,128,256]{2,1,0:T(8,128)S(1)} %get-tuple-element.27), channel_id=1, source_target_pairs={{0,8},{8,16},{16,24},{24,32},{32,40},{40,48},{48,56},{56,64},{64,7... | collective-permute-start | bytes 393224 | tf_op jit(solution)/shard_map/ppermute | solution.py:19
  150.1 11.8 %copy-start.1 = (f32[8,128,256]{2,1,0:T(8,128)}, f32[8,128,256]{2,1,0:T(8,128)S(1)}, u32[]{:S(2)}) copy-start(f32[8,128,256]{2,1,0:T(8,128)S(1)} %fusion.17) | copy-start | bytes 3145732
  150.9 5.7 %collective-permute-start.9 = (f32[1,128,256]{2,1,0:T(8,128)S(1)}, f32[1,128,256]{2,1,0:T(8,128)S(1)}, u32[]{:S(2)}, u32[]{:S(2)}) collective-permute-start(f32[1,128,256]{2,1,0:T(8,128)S(1)} %get-tuple-element.16), channel_id=1, source_target_pairs={{8,0},{16,8},{24,16},{32,24},{40,32},{48,40},{56,48},{64,56},{72,6... | collective-permute-start | bytes 393224 | tf_op jit(solution)/shard_map/ppermute | solution.py:22
  152.8 9.0 %collective-permute-start.10 = (f32[1,128,256]{2,1,0:T(8,128)S(1)}, f32[1,128,256]{2,1,0:T(8,128)S(1)}, u32[]{:S(2)}, u32[]{:S(2)}) collective-permute-start(f32[1,128,256]{2,1,0:T(8,128)S(1)} %get-tuple-element.17), channel_id=1, source_target_pairs={{0,8},{8,16},{16,24},{24,32},{32,40},{40,48},{48,56},{56,64},{64,7... | collective-permute-start | bytes 393224 | tf_op jit(solution)/shard_map/ppermute | solution.py:19
Sparse Core Ops, SparseCore 0:
  33.8 38.9 all-gather.2
  164.4 54.9 all-reduce.1
where the time goes:
time: 229 us
  waiting for transfers between devices  142 us (62%)
  starting transfers between devices  44 us (19%)
  other arithmetic  18.3 us (8%)
  between operations  14.9 us (7%)
  local copies, waits for them, and re-layouts  9.72 us (4%)
    psum x1, waiting for transfers between devices, on_device(): weighted_new = lax.psum(node_weight * force_new, 'node')  55.1 us
    all_gather x1, waiting for transfers between devices, on_device(): shard_piece = lax.all_gather(force_old[None], 'node', axis=0, tiled=True)  38.3 us
    ppermute x5, starting transfers between devices, padded_2(): lax.ppermute(lax.slice_in_dim(block, 0, width, axis=dim), axis, backward)  27.7 us
    ppermute x5, waiting for transfers between devices, padded_2(): lax.ppermute(lax.slice_in_dim(block, block.shape[dim] - width, None, axis...  26.4 us
    ppermute x1, waiting for transfers between devices, shifted_2(): return lax.ppermute(array, axis, pairs)  20.7 us
    ppermute x5, starting transfers between devices, padded_2(): lax.ppermute(lax.slice_in_dim(block, block.shape[dim] - width, None, axis...  13.9 us
    div x4, other arithmetic, on_device(): iterate = (right_side + implicit * neighbour_sum(widened)) / divisor  6.12 us
    slice x10, local copies, waits for them, and re-layouts, neighbour_sum(): total = total + jnp.roll(inner, -1, 2) + jnp.roll(inner, 1, 2)  5.54 us
  transfers between devices with their start and end apart: 13, of which 11 were waited for; matrix products, arithmetic and copies ran while one was open for 2% of the time, Pallas kernels for 0%

commit v1 on v0

--- a/solution.py
+++ b/solution.py
@@ -95,7 +95,7 @@
         iterate = (right_side + implicit * neighbour_sum(widened)) / divisor
     padded_new = padded_2(iterate, (("space", 0),), 1)
     laplace_new, force_new = forcing(iterate, padded_new)
-    weighted_new = lax.psum(node_weight * force_new, "node")
+    weighted_new = jnp.sum(lax.all_gather(node_weight * force_new, axis_name="node"), axis=0)
     end_new = begin_state + time_step * weighted_new
     return (iterate[None, None], end_new[None])
 

time: 229 us -> 216 us (0.943)
  waiting for transfers between devices: 142 us -> 127 us
    psum x1 -> x0, waiting for transfers between devices: 55.1 us -> none  [on_device(): weighted_new = lax.psum(node_weight * force_new, 'node')]
    all_gather x0 -> x1, waiting for transfers between devices: none -> 40.6 us  [on_device(): lax.all_gather(node_weight * force_new, axis_name='node')]
    reduce_sum x0 -> x1, other arithmetic: none -> 2.6 us  [on_device(): jnp.sum(lax.all_gather(node_weight * force_new, axis_name='node'), axis=0)]
  transfers between devices with their start and end apart: 13 -> 13, of which waited for: 11 -> 11; matrix products, arithmetic and copies ran while one was open for 2% -> 3% of each run, Pallas kernels for 0% -> 0%
where the time goes in v1:
time: 216 us; the launch traced here: 215 us
  waiting for transfers between devices  127 us (59%)
  starting transfers between devices  44 us (20%)
  other arithmetic  19.7 us (9%)
  between operations  14.9 us (7%)
  local copies, waits for them, and re-layouts  9.72 us (5%)
    all_gather x1, waiting for transfers between devices, on_device(): lax.all_gather(node_weight * force_new, axis_name='node')  40.6 us
    all_gather x1, waiting for transfers between devices, on_device(): shard_piece = lax.all_gather(force_old[None], 'node', axis=0, tiled=True)  38.3 us
    ppermute x5, starting transfers between devices, padded_2(): lax.ppermute(lax.slice_in_dim(block, 0, width, axis=dim), axis, backward)  27.7 us
    ppermute x5, waiting for transfers between devices, padded_2(): lax.ppermute(lax.slice_in_dim(block, block.shape[dim] - width, None, axis...  26.4 us
    ppermute x1, waiting for transfers between devices, shifted_2(): return lax.ppermute(array, axis, pairs)  20.7 us
    ppermute x5, starting transfers between devices, padded_2(): lax.ppermute(lax.slice_in_dim(block, block.shape[dim] - width, None, axis...  13.9 us
    div x4, other arithmetic, on_device(): iterate = (right_side + implicit * neighbour_sum(widened)) / divisor  6.12 us
    slice x10, local copies, waits for them, and re-layouts, neighbour_sum(): total = total + jnp.roll(inner, -1, 2) + jnp.roll(inner, 1, 2)  5.53 us
  transfers between devices with their start and end apart: 13, of which 11 were waited for; matrix products, arithmetic and copies ran while one was open for 3% of the time, Pallas kernels for 0%

profile of v1, /device:TPU:1, one launch (start us, length us, event | category | flops | bytes accessed | tf_op | source)
XLA Modules:
  0.0 215.5 jit_solution(17102169346021528165)
XLA Ops:
  7.2 1.1 slice_bitcast_fusion.1
  8.3 14.1 %collective-permute-start = (f32[1,128,256]{2,1,0:T(8,128)S(1)}, f32[1,128,256]{2,1,0:T(8,128)S(1)}, u32[]{:S(2)}, u32[]{:S(2)}) collective-permute-start(f32[1,128,256]{2,1,0:T(8,128)S(1)} %get-tuple-element.48), channel_id=1, source_target_pairs={{8,0},{16,8},{24,16},{32,24},{40,32},{48,40},{56,48},{64,56},{72,6... | collective-permute-start | bytes 393224 | tf_op jit(solution)/shard_map/ppermute | solution.py:22
  22.4 1.9 collective-permute-start.1
  24.4 1.4 fusion.63
  25.8 1.9 fusion.62
  27.9 3.6 %collective-permute-done.1 = f32[1,128,256]{2,1,0:T(8,128)S(1)} collective-permute-done((f32[1,128,256]{2,1,0:T(8,128)S(1)}, f32[1,128,256]{2,1,0:T(8,128)S(1)}, u32[]{:S(2)}, u32[]{:S(2)}) %collective-permute-start.1) | collective-permute-done | bytes 131104 | tf_op jit(solution)/shard_map/ppermute | solution.py:19
  31.5 2.2 %fusion = (f32[8,128,256]{2,1,0:T(8,128)}, f32[8,128,256]{2,1,0:T(8,128)}) fusion(f32[1,1,8,128,256]{4,3,2,1,0:T(8,128)S(1)} %copy-done, f32[8,128,255]{2,1,0:T(8,128)S(1)} %get-tuple-element.55, f32[8,128,1]{2,1,0:T(8,128)S(1)} %get-tuple-element.57, f32[8,128,1]{2,1,0:T(8,128)S(1)} %get-tuple-element.56, f32[8,128,255]{2,1,0:T(8,128)S(1)} %get-tuple-element.54, ...), kind=kLoop, calls=%fused_computation.4 | loop fusion | flops 4718592 | bytes 8650752 | tf_op jit(solution)/shard_map/add | solution.py:68
  34.5 38.3 %all-gather.5.cloned.1.call-done = f32[32,128,256]{2,1,0:T(8,128)} async-done(((f32[8,128,256]{2,1,0:T(8,128)}), f32[32,128,256]{2,1,0:T(8,128)}) %all-gather.5.cloned.1.call-update) | async-done | bytes 4194320 | tf_op jit(solution)/shard_map/all_gather | solution.py:83
  72.9 4.1 %multiply_reduce_fusion.1 = (f32[8,128,256]{2,1,0:T(8,128)S(1)}, f32[8,128,256]{2,1,0:T(8,128)}) fusion(f32[4,8,128,256]{3,2,1,0:T(8,128)} %bitcast.31, f32[4]{0:T(128)S(1)} %copy-done.3, f32[4]{0:T(128)S(1)} %dynamic-slice_bitcast_fusion), kind=kLoop, calls=%fused_computation.1 | loop fusion | flops 3670016 | bytes 6291488 | tf_op jit(solution)/shard_map/reduce_sum | solution.py:85
  76.9 1.1 bitcast_add_fusion
  78.0 2.3 %collective-permute-start.2 = (f32[8,128,256]{2,1,0:T(8,128)}, f32[8,128,256]{2,1,0:T(8,128)S(1)}, u32[]{:S(2)}, u32[]{:S(2)}) collective-permute-start(f32[8,128,256]{2,1,0:T(8,128)} %bitcast_add_fusion), channel_id=1, source_target_pairs={{0,1},{2,3},{4,5},{6,7},{8,9},{10,11},{12,13},{14,15},{16,17},{18,... | collective-permute-start | bytes 3145736 | tf_op jit(solution)/shard_map/ppermute | solution.py:30
  82.1 20.7 %collective-permute-done.2 = f32[8,128,256]{2,1,0:T(8,128)S(1)} collective-permute-done((f32[8,128,256]{2,1,0:T(8,128)}, f32[8,128,256]{2,1,0:T(8,128)S(1)}, u32[]{:S(2)}, u32[]{:S(2)}) %collective-permute-start.2) | collective-permute-done | bytes 1048608 | tf_op jit(solution)/shard_map/ppermute | solution.py:30
  102.8 2.5 %add_divide_fusion = (f32[8,128,256]{2,1,0:T(8,128)S(1)}, f32[8,128,256]{2,1,0:T(8,128)S(1)}) fusion(f32[8,128,256]{2,1,0:T(8,128)} %get-tuple-element.7, f32[]{:T(128)S(6)} %add.125, f32[]{:T(128)} %bitcast.6, f32[1,1,8,128,256]{4,3,2,1,0:T(8,128)S(1)} %copy-done, f32[8,128,256]{2,1,0:T(8,128)} %get-tuple-element.3, ...), kind=kLoop, calls=%fused_computation.56 | loop fusion | flops 2621440 | bytes 7340041 | tf_op jit(solution)/shard_map/div | solution.py:95
  106.0 7.8 %collective-permute-start.3 = (f32[1,128,256]{2,1,0:T(8,128)S(1)}, f32[1,128,256]{2,1,0:T(8,128)S(1)}, u32[]{:S(2)}, u32[]{:S(2)}) collective-permute-start(f32[1,128,256]{2,1,0:T(8,128)S(1)} %get-tuple-element.46), channel_id=1, source_target_pairs={{8,0},{16,8},{24,16},{32,24},{40,32},{48,40},{56,48},{64,56},{72,6... | collective-permute-start | bytes 393224 | tf_op jit(solution)/shard_map/ppermute | solution.py:22
  113.9 1.9 collective-permute-start.4
  115.8 7.1 %collective-permute-done.4 = f32[1,128,256]{2,1,0:T(8,128)S(1)} collective-permute-done((f32[1,128,256]{2,1,0:T(8,128)S(1)}, f32[1,128,256]{2,1,0:T(8,128)S(1)}, u32[]{:S(2)}, u32[]{:S(2)}) %collective-permute-start.4) | collective-permute-done | bytes 131104 | tf_op jit(solution)/shard_map/ppermute | solution.py:19
  122.9 1.2 fusion.33
  124.9 1.9 collective-permute-start.5
  126.8 3.4 %collective-permute-start.6 = (f32[1,128,256]{2,1,0:T(8,128)S(1)}, f32[1,128,256]{2,1,0:T(8,128)S(1)}, u32[]{:S(2)}, u32[]{:S(2)}) collective-permute-start(f32[1,128,256]{2,1,0:T(8,128)S(1)} %get-tuple-element.37), channel_id=1, source_target_pairs={{0,8},{8,16},{16,24},{24,32},{32,40},{40,48},{48,56},{56,64},{64,7... | collective-permute-start | bytes 393224 | tf_op jit(solution)/shard_map/ppermute | solution.py:19
  130.6 5.2 %collective-permute-done.6 = f32[1,128,256]{2,1,0:T(8,128)S(1)} collective-permute-done((f32[1,128,256]{2,1,0:T(8,128)S(1)}, f32[1,128,256]{2,1,0:T(8,128)S(1)}, u32[]{:S(2)}, u32[]{:S(2)}) %collective-permute-start.6) | collective-permute-done | bytes 131104 | tf_op jit(solution)/shard_map/ppermute | solution.py:19
  135.9 1.2 fusion.25
  137.9 1.9 collective-permute-start.7
  139.8 3.4 %collective-permute-start.8 = (f32[1,128,256]{2,1,0:T(8,128)S(1)}, f32[1,128,256]{2,1,0:T(8,128)S(1)}, u32[]{:S(2)}, u32[]{:S(2)}) collective-permute-start(f32[1,128,256]{2,1,0:T(8,128)S(1)} %get-tuple-element.27), channel_id=1, source_target_pairs={{0,8},{8,16},{16,24},{24,32},{32,40},{40,48},{48,56},{56,64},{64,7... | collective-permute-start | bytes 393224 | tf_op jit(solution)/shard_map/ppermute | solution.py:19
  143.6 5.2 %collective-permute-done.8 = f32[1,128,256]{2,1,0:T(8,128)S(1)} collective-permute-done((f32[1,128,256]{2,1,0:T(8,128)S(1)}, f32[1,128,256]{2,1,0:T(8,128)S(1)}, u32[]{:S(2)}, u32[]{:S(2)}) %collective-permute-start.8) | collective-permute-done | bytes 131104 | tf_op jit(solution)/shard_map/ppermute | solution.py:19
  148.8 1.2 fusion.17
  150.9 1.9 collective-permute-start.9
  152.8 3.4 %collective-permute-start.10 = (f32[1,128,256]{2,1,0:T(8,128)S(1)}, f32[1,128,256]{2,1,0:T(8,128)S(1)}, u32[]{:S(2)}, u32[]{:S(2)}) collective-permute-start(f32[1,128,256]{2,1,0:T(8,128)S(1)} %get-tuple-element.17), channel_id=1, source_target_pairs={{0,8},{8,16},{16,24},{24,32},{32,40},{40,48},{48,56},{56,64},{64,7... | collective-permute-start | bytes 393224 | tf_op jit(solution)/shard_map/ppermute | solution.py:19
  156.6 5.2 %collective-permute-done.10 = f32[1,128,256]{2,1,0:T(8,128)S(1)} collective-permute-done((f32[1,128,256]{2,1,0:T(8,128)S(1)}, f32[1,128,256]{2,1,0:T(8,128)S(1)}, u32[]{:S(2)}, u32[]{:S(2)}) %collective-permute-start.10) | collective-permute-done | bytes 131104 | tf_op jit(solution)/shard_map/ppermute | solution.py:19
  161.8 2.4 %fusion.2 = f32[8,128,256]{2,1,0:T(8,128)} fusion(f32[8,128,256]{2,1,0:T(8,128)S(1)} %fusion.17, f32[1,128,256]{2,1,0:T(8,128)S(1)} %collective-permute-done.10, f32[1,128,256]{2,1,0:T(8,128)S(1)} %collective-permute-done.9, f32[8,1,256]{2,1,0:T(1,128)S(1)} %get-tuple-element.13, f32[8,127,256]{2,1,0:T(8,128)S(1)} %get-tuple-element.15, ...), kind=kLoop, calls=%fused_computation.6 | loop fusion | flops 4980736 | bytes 6553604 | tf_op jit(solution)/shard_map/mul | solution.py:98
  164.3 40.6 %all-gather.7.cloned.1.call-done = f32[32,128,256]{2,1,0:T(8,128)} async-done(((f32[8,128,256]{2,1,0:T(8,128)}), f32[32,128,256]{2,1,0:T(8,128)}) %all-gather.7.cloned.1.call-update) | async-done | bytes 4194320 | tf_op jit(solution)/shard_map/all_gather | solution.py:98
  204.9 2.6 %reduce_sum.29 = f32[8,128,256]{2,1,0:T(8,128)S(1)} reduce(f32[4,8,128,256]{3,2,1,0:T(8,128)} %bitcast.32, f32[]{:T(128)} %constant.8.clone.1), dimensions={0}, to_apply=%region_2.3 | reduce | flops 786432 | bytes 5242884 | tf_op jit(solution)/shard_map/reduce_sum | solution.py:98
  207.5 1.2 add_bitcast_fusion
  (44 shorter events, 6.6 us)
Async XLA Ops:
  7.2 20.5 %copy-start = (f32[1,1,8,128,256]{4,3,2,1,0:T(8,128)S(1)}, f32[1,1,8,128,256]{4,3,2,1,0:T(8,128)}, u32[]{:S(2)}) copy-start(f32[1,1,8,128,256]{4,3,2,1,0:T(8,128)} %param.6) | copy-start | bytes 3145732
  7.2 65.7 %all-gather.5.cloned.1.call-start = ((), (), s32[]{:S(2)}) async-start(), calls=%async_computation | async-start | bytes 5242880 | tf_op jit(solution)/shard_map/all_gather | solution.py:83
  8.3 19.6 %collective-permute-start = (f32[1,128,256]{2,1,0:T(8,128)S(1)}, f32[1,128,256]{2,1,0:T(8,128)S(1)}, u32[]{:S(2)}, u32[]{:S(2)}) collective-permute-start(f32[1,128,256]{2,1,0:T(8,128)S(1)} %get-tuple-element.48), channel_id=1, source_target_pairs={{8,0},{16,8},{24,16},{32,24},{40,32},{48,40},{56,48},{64,56},{72,6... | collective-permute-start | bytes 393224 | tf_op jit(solution)/shard_map/ppermute | solution.py:22
  22.4 9.0 %collective-permute-start.1 = (f32[1,128,256]{2,1,0:T(8,128)S(1)}, f32[1,128,256]{2,1,0:T(8,128)S(1)}, u32[]{:S(2)}, u32[]{:S(2)}) collective-permute-start(f32[1,128,256]{2,1,0:T(8,128)S(1)} %get-tuple-element.49), channel_id=1, source_target_pairs={{0,8},{8,16},{16,24},{24,32},{32,40},{40,48},{48,56},{56,64},{64,7... | collective-permute-start | bytes 393224 | tf_op jit(solution)/shard_map/ppermute | solution.py:19
  31.5 41.4 %copy-start.3 = (f32[4]{0:T(128)S(1)}, f32[4]{0:T(128)}, u32[]{:S(2)}) copy-start(f32[4]{0:T(128)} %constant.30.clone) | copy-start | bytes 52
  33.7 43.2 %copy-start.2 = (f32[1,8,128,256]{3,2,1,0:T(8,128)S(1)}, f32[1,8,128,256]{3,2,1,0:T(8,128)}, u32[]{:S(2)}) copy-start(f32[1,8,128,256]{3,2,1,0:T(8,128)} %param.5) | copy-start | bytes 3145732
  33.7 171.2 %all-gather.7.cloned.1.call-start = ((), (), s32[]{:S(2)}) async-start(), calls=%async_computation.1 | async-start | bytes 5242880 | tf_op jit(solution)/shard_map/all_gather | solution.py:98
  72.9 8.1 %copy-start.4 = (f32[4]{0:T(128)S(1)}, f32[4]{0:T(128)}, u32[]{:S(2)}) copy-start(f32[4]{0:T(128)} %constant.29.clone) | copy-start | bytes 52
  78.0 24.7 %collective-permute-start.2 = (f32[8,128,256]{2,1,0:T(8,128)}, f32[8,128,256]{2,1,0:T(8,128)S(1)}, u32[]{:S(2)}, u32[]{:S(2)}) collective-permute-start(f32[8,128,256]{2,1,0:T(8,128)} %bitcast_add_fusion), channel_id=1, source_target_pairs={{0,1},{2,3},{4,5},{6,7},{8,9},{10,11},{12,13},{14,15},{16,17},{18,... | collective-permute-start | bytes 3145736 | tf_op jit(solution)/shard_map/ppermute | solution.py:30
  106.0 9.8 %collective-permute-start.3 = (f32[1,128,256]{2,1,0:T(8,128)S(1)}, f32[1,128,256]{2,1,0:T(8,128)S(1)}, u32[]{:S(2)}, u32[]{:S(2)}) collective-permute-start(f32[1,128,256]{2,1,0:T(8,128)S(1)} %get-tuple-element.46), channel_id=1, source_target_pairs={{8,0},{16,8},{24,16},{32,24},{40,32},{48,40},{56,48},{64,56},{72,6... | collective-permute-start | bytes 393224 | tf_op jit(solution)/shard_map/ppermute | solution.py:22
  113.9 9.0 %collective-permute-start.4 = (f32[1,128,256]{2,1,0:T(8,128)S(1)}, f32[1,128,256]{2,1,0:T(8,128)S(1)}, u32[]{:S(2)}, u32[]{:S(2)}) collective-permute-start(f32[1,128,256]{2,1,0:T(8,128)S(1)} %get-tuple-element.47), channel_id=1, source_target_pairs={{0,8},{8,16},{16,24},{24,32},{32,40},{40,48},{48,56},{56,64},{64,7... | collective-permute-start | bytes 393224 | tf_op jit(solution)/shard_map/ppermute | solution.py:19
  124.9 5.7 %collective-permute-start.5 = (f32[1,128,256]{2,1,0:T(8,128)S(1)}, f32[1,128,256]{2,1,0:T(8,128)S(1)}, u32[]{:S(2)}, u32[]{:S(2)}) collective-permute-start(f32[1,128,256]{2,1,0:T(8,128)S(1)} %get-tuple-element.36), channel_id=1, source_target_pairs={{8,0},{16,8},{24,16},{32,24},{40,32},{48,40},{56,48},{64,56},{72,6... | collective-permute-start | bytes 393224 | tf_op jit(solution)/shard_map/ppermute | solution.py:22
  126.8 9.0 %collective-permute-start.6 = (f32[1,128,256]{2,1,0:T(8,128)S(1)}, f32[1,128,256]{2,1,0:T(8,128)S(1)}, u32[]{:S(2)}, u32[]{:S(2)}) collective-permute-start(f32[1,128,256]{2,1,0:T(8,128)S(1)} %get-tuple-element.37), channel_id=1, source_target_pairs={{0,8},{8,16},{16,24},{24,32},{32,40},{40,48},{48,56},{56,64},{64,7... | collective-permute-start | bytes 393224 | tf_op jit(solution)/shard_map/ppermute | solution.py:19
  137.9 5.7 %collective-permute-start.7 = (f32[1,128,256]{2,1,0:T(8,128)S(1)}, f32[1,128,256]{2,1,0:T(8,128)S(1)}, u32[]{:S(2)}, u32[]{:S(2)}) collective-permute-start(f32[1,128,256]{2,1,0:T(8,128)S(1)} %get-tuple-element.26), channel_id=1, source_target_pairs={{8,0},{16,8},{24,16},{32,24},{40,32},{48,40},{56,48},{64,56},{72,6... | collective-permute-start | bytes 393224 | tf_op jit(solution)/shard_map/ppermute | solution.py:22
  139.8 9.0 %collective-permute-start.8 = (f32[1,128,256]{2,1,0:T(8,128)S(1)}, f32[1,128,256]{2,1,0:T(8,128)S(1)}, u32[]{:S(2)}, u32[]{:S(2)}) collective-permute-start(f32[1,128,256]{2,1,0:T(8,128)S(1)} %get-tuple-element.27), channel_id=1, source_target_pairs={{0,8},{8,16},{16,24},{24,32},{32,40},{40,48},{48,56},{56,64},{64,7... | collective-permute-start | bytes 393224 | tf_op jit(solution)/shard_map/ppermute | solution.py:19
  150.1 11.8 %copy-start.1 = (f32[8,128,256]{2,1,0:T(8,128)}, f32[8,128,256]{2,1,0:T(8,128)S(1)}, u32[]{:S(2)}) copy-start(f32[8,128,256]{2,1,0:T(8,128)S(1)} %fusion.17) | copy-start | bytes 3145732
  150.9 5.7 %collective-permute-start.9 = (f32[1,128,256]{2,1,0:T(8,128)S(1)}, f32[1,128,256]{2,1,0:T(8,128)S(1)}, u32[]{:S(2)}, u32[]{:S(2)}) collective-permute-start(f32[1,128,256]{2,1,0:T(8,128)S(1)} %get-tuple-element.16), channel_id=1, source_target_pairs={{8,0},{16,8},{24,16},{32,24},{40,32},{48,40},{56,48},{64,56},{72,6... | collective-permute-start | bytes 393224 | tf_op jit(solution)/shard_map/ppermute | solution.py:22
  152.8 9.0 %collective-permute-start.10 = (f32[1,128,256]{2,1,0:T(8,128)S(1)}, f32[1,128,256]{2,1,0:T(8,128)S(1)}, u32[]{:S(2)}, u32[]{:S(2)}) collective-permute-start(f32[1,128,256]{2,1,0:T(8,128)S(1)} %get-tuple-element.17), channel_id=1, source_target_pairs={{0,8},{8,16},{16,24},{24,32},{32,40},{40,48},{48,56},{56,64},{64,7... | collective-permute-start | bytes 393224 | tf_op jit(solution)/shard_map/ppermute | solution.py:19
Sparse Core Ops, SparseCore 0:
  33.8 38.9 all-gather.4
  164.4 40.4 all-gather.6
